TPU v7x, 32 devices: a whole 2x2x4 slice. The times are simulated.
32 devices in a mesh: groups: 2 (over y), seq: 4 (over z), mp: 2 (over x), sub: 2 (over core).
Axes of the slice: x: 2, y: 2, z: 4, core: 2. Of those that a mesh axis runs over, the one named last changes fastest.
Arguments:
- seq_in: bfloat16 [4096, 1536], P(('groups', 'seq'), ('mp', 'sub')), parts along dimension 0, may hold values from -48 to 48
- conv_gain: float32 [3, 1536], replicated, may hold values from 0.1 to 1.9
- conv_weight: bfloat16 [3, 3, 1536, 1536], P(None, None, None, ('mp', 'sub')), may hold values from -0.09375 to 0.09375
- w_q: bfloat16 [1536, 1024], P(None, 'mp'), may hold values from -0.102062073 to 0.102062073
- w_k: bfloat16 [1536, 1024], P(None, 'mp'), may hold values from -0.102062073 to 0.102062073
- w_v: bfloat16 [1536, 1024], P(None, 'mp'), may hold values from -0.15625 to 0.15625
- w_o: bfloat16 [1024, 1536], P('mp'), may hold values from -0.1875 to 0.1875
Outputs:
- seq_out: bfloat16 [4096, 1536], P(('groups', 'seq', 'sub'), 'mp'), parts along dimension 0
There are 2 independent parts, one for each index of `groups`. A program takes and returns all parts, laid end to end along the dimension named above; an argument that names none is the same for every part. Nothing has to cross between parts.
All inputs are finite; a program needn't handle non-finite values.
Results may differ from a plain program's by a relative error of at most 0.015.
Values may be sent and summed in bfloat16 or wider, within the bound.
No kernel may reach another device: no remote copies, remote signals or barrier semaphores. Data moves between devices by JAX's collectives and lax.ppermute only.
A program may use at most 128 MiB of HBM per device.

v0:
```python
import math
import jax
import jax.numpy as jnp
from jax import lax
from jax.sharding import PartitionSpec as P

HEAD = 128
LAYERS = 3
BINS_DEV = 512


def passed_along(x, axis, by):
    devices = lax.axis_size(axis)
    pairs = [(i, i + by) for i in range(devices) if 0 <= i + by < devices]
    return lax.ppermute(x, axis, pairs)


def tower_section(stream_shard, gain_row, weight_taps, dilation):
    rows_here = stream_shard.shape[0]
    gathered = lax.all_gather(stream_shard, ("mp", "sub"), axis=1, tiled=True)
    widened = gathered.astype(jnp.float32)
    normed = (
        widened * lax.rsqrt(jnp.mean(widened * widened, axis=1, keepdims=True) + 1e-06) * gain_row
    )
    hidden = jax.nn.gelu(normed).astype(jnp.bfloat16)
    tap_terms = jnp.einsum("rc,jco->jro", hidden, weight_taps, preferred_element_type=jnp.float32)
    span_rows = min(dilation, rows_here)
    hop_count = max(dilation // rows_here, 1)
    lower_part = passed_along(
        tap_terms[0, rows_here - span_rows :].astype(jnp.bfloat16), "seq", hop_count
    ).astype(jnp.float32)
    upper_part = passed_along(
        tap_terms[2, :span_rows].astype(jnp.bfloat16), "seq", -hop_count
    ).astype(jnp.float32)
    before = jnp.concatenate([lower_part, tap_terms[0, : rows_here - span_rows]], axis=0)
    after = jnp.concatenate([tap_terms[2, span_rows:], upper_part], axis=0)
    return (stream_shard.astype(jnp.float32) + before + tap_terms[1] + after).astype(jnp.bfloat16)


def per_device(seq_in, conv_gain, conv_weight, w_q, w_k, w_v, w_o):
    rows_here = seq_in.shape[0]
    dilations = (BINS_DEV // 4, BINS_DEV, 2 * BINS_DEV)
    stream = seq_in
    for section_index in range(LAYERS):
        stream = tower_section(
            stream, conv_gain[section_index], conv_weight[section_index], dilations[section_index]
        )
    query_rows = rows_here // lax.axis_size("sub")
    mp_width = w_o.shape[1] // lax.axis_size("mp")
    widest = lax.all_gather(stream, ("mp", "sub"), axis=1, tiled=True)
    query_inputs = lax.dynamic_slice_in_dim(
        widest, lax.axis_index("sub") * query_rows, query_rows, 0
    )
    residual_part = lax.dynamic_slice_in_dim(
        query_inputs, lax.axis_index("mp") * mp_width, mp_width, 1
    )
    heads_here = w_q.shape[1] // HEAD
    queries = (
        jnp.dot(query_inputs, w_q, preferred_element_type=jnp.float32)
        .astype(jnp.bfloat16)
        .reshape(query_rows, heads_here, HEAD)
    )
    keys = (
        jnp.dot(query_inputs, w_k, preferred_element_type=jnp.float32)
        .astype(jnp.bfloat16)
        .reshape(query_rows, heads_here, HEAD)
    )
    values = (
        jnp.dot(query_inputs, w_v, preferred_element_type=jnp.float32)
        .astype(jnp.bfloat16)
        .reshape(query_rows, heads_here, HEAD)
    )
    score_scale = 1.0 / math.sqrt(HEAD)
    running_top = jnp.full((heads_here, query_rows), -1e30, jnp.float32)
    running_numer = jnp.zeros((query_rows, heads_here, HEAD), jnp.float32)
    key_rows = lax.all_gather(keys, ("seq", "sub"), axis=0, tiled=True)
    value_rows = lax.all_gather(values, ("seq", "sub"), axis=0, tiled=True)
    scores = (
        jnp.einsum("qhe,khe->hqk", queries, key_rows, preferred_element_type=jnp.float32)
        * score_scale
    )
    new_top = jnp.maximum(running_top, jnp.max(scores, axis=-1))
    expw = jnp.exp(scores - new_top[:, :, None])
    factor = jnp.exp(running_top - new_top)
    new_denom = jnp.sum(expw, axis=-1)
    contrib = jnp.einsum(
        "hqk,khe->qhe", expw.astype(jnp.bfloat16), value_rows, preferred_element_type=jnp.float32
    )
    new_numer = running_numer * factor.T[:, :, None] + contrib
    attended = (
        (new_numer / new_denom.T[:, :, None])
        .astype(jnp.bfloat16)
        .reshape(query_rows, heads_here * HEAD)
    )
    column_weight = lax.all_to_all(w_o, "mp", split_axis=1, concat_axis=0, tiled=True)
    every_head = lax.all_gather(attended, "mp", axis=1, tiled=True)
    shares = jnp.dot(every_head, column_weight, preferred_element_type=jnp.float32)
    return (residual_part.astype(jnp.float32) + shares).astype(jnp.bfloat16)


def solution(mesh):
    placed = (
        P(("groups", "seq"), ("mp", "sub")),
        P(),
        P(None, None, None, ("mp", "sub")),
        P(None, "mp"),
        P(None, "mp"),
        P(None, "mp"),
        P("mp", None),
    )
    return jax.shard_map(
        per_device,
        mesh=mesh,
        in_specs=placed,
        out_specs=P(("groups", "seq", "sub"), "mp"),
        check_vma=False,
    )
```

profile of v0, /device:TPU:8, one launch (start us, length us, event | category | flops | bytes accessed | tf_op | source)
XLA Modules:
  0.0 252.6 jit_solution(15815357984765979070)
XLA Ops:
  6.5 0.0 copy-start
  6.5 0.0 all-gather.7.cloned.1.call-start
  6.5 0.7 all-gather.7.cloned.1.call-update
  7.3 0.0 all-gather.9.cloned.1.call-start
  7.3 0.9 slice_reduce_fusion
  8.2 21.5 %all-gather.7.cloned.1.call-done = bf16[512,1536]{1,0:T(8,128)(2,1)} async-done(((bf16[512,384]{1,0:T(8,128)(2,1)}), bf16[512,1536]{1,0:T(8,128)(2,1)}) %all-gather.7.cloned.1.call-update) | async-done | bytes 1572880 | tf_op jit(solution)/shard_map/all_gather | solution.py:20
  29.8 1.8 fusion.15
  31.6 5.6 %fusion.124 = (bf16[3,512,384]{2,1,0:T(8,128)(2,1)S(1)}, f32[3,512,384]{2,1,0:T(8,128)S(1)}) fusion(bf16[3,3,1536,384]{3,2,1,0:T(8,128)(2,1)} %param.9, bf16[512,1536]{1,0:T(8,128)(2,1)} %all-gather.7.cloned.1.call-done, f32[1536]{0:T(1024)S(1)} %get-tuple-element.6, f32[512]{0:T(512)S(1)} %add_rsqrt_fusion.2), kind=kOutput, calls=%fused_computation.142 | convolution fusion | flops 1821966336 | bytes 8658944 | tf_op jit(solution)/shard_map/rc,jco->jro/dot_general | solution.py:26
  37.1 0.0 copy-start.6
  37.2 3.5 %collective-permute-start = (bf16[128,384]{1,0:T(8,128)(2,1)S(1)}, bf16[128,384]{1,0:T(8,128)(2,1)S(1)}, u32[]{:S(2)}, u32[]{:S(2)}) collective-permute-start(bf16[128,384]{1,0:T(8,128)(2,1)S(1)} %get-tuple-element.15), channel_id=1, source_target_pairs={{0,4},{4,8},{8,12},{1,5},{5,9},{9,13},{2,6},{6,10},{10,14},{3,7},{... | collective-permute-start | bytes 294920 | tf_op jit(solution)/shard_map/ppermute | solution.py:15
  40.7 2.5 collective-permute-start.1
  43.2 0.1 slice_bitcast_fusion.3
  43.3 0.9 collective-permute-done
  44.2 3.1 %collective-permute-done.1 = bf16[128,384]{1,0:T(8,128)(2,1)S(1)} collective-permute-done((bf16[128,384]{1,0:T(8,128)(2,1)S(1)}, bf16[128,384]{1,0:T(8,128)(2,1)S(1)}, u32[]{:S(2)}, u32[]{:S(2)}) %collective-permute-start.1) | collective-permute-done | bytes 98336 | tf_op jit(solution)/shard_map/ppermute | solution.py:15
  47.3 0.0 copy-done.6
  47.3 0.9 fusion.101
  48.2 0.0 all-gather.9.cloned.1.call-update
  48.3 0.0 all-gather.11.cloned.1.call-start
  48.3 18.8 %all-gather.9.cloned.1.call-done = bf16[512,1536]{1,0:T(8,128)(2,1)} async-done(((bf16[512,384]{1,0:T(8,128)(2,1)}), bf16[512,1536]{1,0:T(8,128)(2,1)}) %all-gather.9.cloned.1.call-update) | async-done | bytes 1572880 | tf_op jit(solution)/shard_map/all_gather | solution.py:20
  67.1 1.8 fusion.24
  68.9 0.0 copy-start.3
  68.9 5.6 %fusion.125 = (bf16[3,512,384]{2,1,0:T(8,128)(2,1)S(1)}, f32[3,512,384]{2,1,0:T(8,128)S(1)}) fusion(bf16[3,3,1536,384]{3,2,1,0:T(8,128)(2,1)} %param.9, bf16[512,1536]{1,0:T(8,128)(2,1)} %all-gather.9.cloned.1.call-done, f32[1536]{0:T(1024)S(1)} %get-tuple-element.7, f32[512]{0:T(512)S(1)} %add_rsqrt_fusion.1), kind=kOutput, calls=%fused_computation.143 | convolution fusion | flops 1821966336 | bytes 8658944 | tf_op jit(solution)/shard_map/rc,jco->jro/dot_general | solution.py:26
  74.6 0.1 slice_bitcast_fusion.8
  74.7 3.4 %collective-permute-start.2 = (bf16[512,384]{1,0:T(8,128)(2,1)S(1)}, bf16[512,384]{1,0:T(8,128)(2,1)S(1)}, u32[]{:S(2)}, u32[]{:S(2)}) collective-permute-start(bf16[512,384]{1,0:T(8,128)(2,1)S(1)} %get-tuple-element.12), channel_id=1, source_target_pairs={{0,4},{4,8},{8,12},{1,5},{5,9},{9,13},{2,6},{6,10},{10,14},{3,7},{... | collective-permute-start | bytes 1179656 | tf_op jit(solution)/shard_map/ppermute | solution.py:15
  78.1 2.5 collective-permute-start.3
  80.6 7.3 %collective-permute-done.2 = bf16[512,384]{1,0:T(8,128)(2,1)S(1)} collective-permute-done((bf16[512,384]{1,0:T(8,128)(2,1)S(1)}, bf16[512,384]{1,0:T(8,128)(2,1)S(1)}, u32[]{:S(2)}, u32[]{:S(2)}) %collective-permute-start.2) | collective-permute-done | bytes 393248 | tf_op jit(solution)/shard_map/ppermute | solution.py:15
  87.8 3.1 %collective-permute-done.3 = bf16[512,384]{1,0:T(8,128)(2,1)S(1)} collective-permute-done((bf16[512,384]{1,0:T(8,128)(2,1)S(1)}, bf16[512,384]{1,0:T(8,128)(2,1)S(1)}, u32[]{:S(2)}, u32[]{:S(2)}) %collective-permute-start.3) | collective-permute-done | bytes 393248 | tf_op jit(solution)/shard_map/ppermute | solution.py:15
  90.9 1.0 fusion.98
  91.9 0.0 all-gather.11.cloned.1.call-update
  91.9 0.0 all-gather.13.cloned.1.call-start
  92.0 18.8 %all-gather.11.cloned.1.call-done = bf16[512,1536]{1,0:T(8,128)(2,1)} async-done(((bf16[512,384]{1,0:T(8,128)(2,1)}), bf16[512,1536]{1,0:T(8,128)(2,1)}) %all-gather.11.cloned.1.call-update) | async-done | bytes 1572880 | tf_op jit(solution)/shard_map/all_gather | solution.py:20
  110.8 1.8 fusion.33
  112.6 0.0 copy-start.4
  112.6 5.6 %fusion.126 = (bf16[3,512,384]{2,1,0:T(8,128)(2,1)S(1)}, f32[3,512,384]{2,1,0:T(8,128)S(1)}) fusion(bf16[3,3,1536,384]{3,2,1,0:T(8,128)(2,1)} %param.9, bf16[512,1536]{1,0:T(8,128)(2,1)} %all-gather.11.cloned.1.call-done, f32[1536]{0:T(1024)S(1)} %get-tuple-element.5, f32[512]{0:T(512)S(1)} %add_rsqrt_fusion), kind=kOutput, calls=%fused_computation.144 | convolution fusion | flops 1821966336 | bytes 8658944 | tf_op jit(solution)/shard_map/rc,jco->jro/dot_general | solution.py:26
  118.3 0.1 slice_bitcast_fusion.6
  118.4 4.3 %collective-permute-start.4 = (bf16[512,384]{1,0:T(8,128)(2,1)S(1)}, bf16[512,384]{1,0:T(8,128)(2,1)S(1)}, u32[]{:S(2)}, u32[]{:S(2)}) collective-permute-start(bf16[512,384]{1,0:T(8,128)(2,1)S(1)} %get-tuple-element.10), channel_id=1, source_target_pairs={{0,8},{4,12},{1,9},{5,13},{2,10},{6,14},{3,11},{7,15},{16,24},{20,... | collective-permute-start | bytes 1179656 | tf_op jit(solution)/shard_map/ppermute | solution.py:15
  122.7 1.3 collective-permute-start.5
  124.0 15.8 %collective-permute-done.4 = bf16[512,384]{1,0:T(8,128)(2,1)S(1)} collective-permute-done((bf16[512,384]{1,0:T(8,128)(2,1)S(1)}, bf16[512,384]{1,0:T(8,128)(2,1)S(1)}, u32[]{:S(2)}, u32[]{:S(2)}) %collective-permute-start.4) | collective-permute-done | bytes 393248 | tf_op jit(solution)/shard_map/ppermute | solution.py:15
  139.8 0.0 collective-permute-done.5
  139.8 1.0 fusion.95
  140.8 0.0 all-gather.13.cloned.1.call-update
  140.8 0.0 all-gather.15.cloned.1.call-start
  140.9 0.0 copy-start.5
  140.9 22.0 %all-gather.13.cloned.1.call-done = bf16[512,1536]{1,0:T(8,128)(2,1)} async-done(((bf16[512,384]{1,0:T(8,128)(2,1)}), bf16[512,1536]{1,0:T(8,128)(2,1)}) %all-gather.13.cloned.1.call-update) | async-done | bytes 1572880 | tf_op jit(solution)/shard_map/all_gather | solution.py:50
  162.9 1.7 fusion.86
  164.6 0.8 copy.29
  165.4 0.0 all-gather.15.cloned.1.call-update
  165.4 0.2 all-gather.17.cloned.1.call-start
  165.6 2.2 convolution_convert_fusion
  167.9 0.8 copy.19
  168.7 0.0 all-gather.17.cloned.1.call-update
  168.7 1.6 copy.17
  170.3 3.7 %all-to-all-start = ((bf16[512,2,768]{0,2,1:T(8,128)(2,1)}), bf16[512,2,768]{0,2,1:T(8,128)(2,1)S(1)}, u32[]{:S(2)}, u32[]{:S(2)}) async-start(bf16[512,2,768]{0,2,1:T(8,128)(2,1)} %bitcast.118), calls=%async_computation | async-start | bytes 3145728 | tf_op jit(solution)/shard_map/all_to_all | solution.py:95
  174.0 19.9 %all-to-all-done = bf16[512,2,768]{0,2,1:T(8,128)(2,1)S(1)} async-done(((bf16[512,2,768]{0,2,1:T(8,128)(2,1)}), bf16[512,2,768]{0,2,1:T(8,128)(2,1)S(1)}, u32[]{:S(2)}, u32[]{:S(2)}) %all-to-all-start) | async-done | bytes 1572896 | tf_op jit(solution)/shard_map/all_to_all | solution.py:95
  193.9 1.6 copy.18
  195.5 2.2 fusion.85
  197.8 0.0 all-gather.15.cloned.1.call-done
  197.8 2.9 %multiply_reduce_fusion = (f32[4,256]{1,0:T(4,128)S(1)}, f32[4,256,2048]{2,1,0:T(8,128)S(1)}) fusion(bf16[2048,4,128]{2,0,1:T(8,128)(2,1)} %all-gather.15.cloned.1.call-done, bf16[32,4,8,128]{3,2,1,0:T(8,128)(2,1)S(1)} %fusion.85), kind=kOutput, calls=%fused_computation.1 | convolution fusion | flops 541064192 | bytes 10752000 | tf_op jit(solution)/shard_map/qhe,khe->hqk/dot_general | solution.py:79
  200.7 3.2 %copy-done.1 = f32[4,256,2048]{2,1,0:T(8,128)} copy-done((f32[4,256,2048]{2,1,0:T(8,128)}, f32[4,256,2048]{2,1,0:T(8,128)S(1)}, u32[]{:S(2)}) %copy-start.1) | copy-done | bytes 8388632
  204.0 1.6 fusion
  205.6 22.7 %all-gather.17.cloned.1.call-done = bf16[2048,4,128]{0,2,1:T(8,128)(2,1)} async-done(((bf16[256,4,128]{0,2,1:T(8,128)(2,1)}), bf16[2048,4,128]{0,2,1:T(8,128)(2,1)}) %all-gather.17.cloned.1.call-update) | async-done | bytes 2097168 | tf_op jit(solution)/shard_map/all_gather | solution.py:77
  228.3 5.9 %fusion.90 = bf16[256,4,128]{0,2,1:T(8,128)(2,1)S(1)} fusion(bf16[2048,4,128]{0,2,1:T(8,128)(2,1)} %all-gather.17.cloned.1.call-done, f32[4,256,2048]{2,1,0:T(8,128)} %copy-done.1, f32[4,256]{1,0:T(4,128)S(1)} %get-tuple-element.17, f32[256,4]{0,1:T(4,128)S(1)} %bitcast.123, f32[256,4]{0,1:T(4,128)S(1)} %get-tuple-element.16), kind=kOutput, calls=%fused_computation.89 | convolution fusion | flops 543555584 | bytes 10760192 | tf_op jit(solution)/shard_map/hqk,khe->qhe/dot_general | solution.py:86
  234.2 9.1 %all_gather.27 = bf16[256,1024]{0,1:T(8,128)(2,1)S(1)} all-gather(bf16[256,512]{0,1:T(8,128)(2,1)S(1)} %bitcast.122), channel_id=1, replica_groups=mesh['groups'=2,'seq'=4,'mp'=2,'sub'=2] {'mp'}, dimensions={1}, use_global_device_ids=true | all-gather | bytes 786432 | tf_op jit(solution)/shard_map/all_gather | solution.py:96
  243.4 2.4 fusion.78
  (14 shorter events, 0.1 us)
Async XLA Ops:
  6.5 156.4 %copy-start = (bf16[1536,512]{1,0:T(8,128)(2,1)S(1)}, bf16[1536,512]{1,0:T(8,128)(2,1)}, u32[]{:S(2)}) copy-start(bf16[1536,512]{1,0:T(8,128)(2,1)} %param.11) | copy-start | bytes 4718596
  6.5 23.2 %all-gather.7.cloned.1.call-start = ((), (), s32[]{:S(2)}) async-start(), calls=%async_computation.1 | async-start | bytes 1966080 | tf_op jit(solution)/shard_map/all_gather | solution.py:20
  7.3 59.9 %all-gather.9.cloned.1.call-start = ((), (), s32[]{:S(2)}) async-start(), calls=%async_computation.2 | async-start | bytes 1966080 | tf_op jit(solution)/shard_map/all_gather | solution.py:20
  37.1 10.1 %copy-start.6 = (bf16[512,384]{1,0:T(8,128)(2,1)S(1)}, bf16[512,384]{1,0:T(8,128)(2,1)}, u32[]{:S(2)}) copy-start(bf16[512,384]{1,0:T(8,128)(2,1)} %param.7) | copy-start | bytes 1179652
  37.2 7.0 %collective-permute-start = (bf16[128,384]{1,0:T(8,128)(2,1)S(1)}, bf16[128,384]{1,0:T(8,128)(2,1)S(1)}, u32[]{:S(2)}, u32[]{:S(2)}) collective-permute-start(bf16[128,384]{1,0:T(8,128)(2,1)S(1)} %get-tuple-element.15), channel_id=1, source_target_pairs={{0,4},{4,8},{8,12},{1,5},{5,9},{9,13},{2,6},{6,10},{10,14},{3,7},{... | collective-permute-start | bytes 294920 | tf_op jit(solution)/shard_map/ppermute | solution.py:15
  40.7 6.6 %collective-permute-start.1 = (bf16[128,384]{1,0:T(8,128)(2,1)S(1)}, bf16[128,384]{1,0:T(8,128)(2,1)S(1)}, u32[]{:S(2)}, u32[]{:S(2)}) collective-permute-start(bf16[128,384]{1,0:T(8,128)(2,1)S(1)} %get-tuple-element.14), channel_id=1, source_target_pairs={{4,0},{8,4},{12,8},{5,1},{9,5},{13,9},{6,2},{10,6},{14,10},{7,3},{... | collective-permute-start | bytes 294920 | tf_op jit(solution)/shard_map/ppermute | solution.py:15
  48.3 62.5 %all-gather.11.cloned.1.call-start = ((), (), s32[]{:S(2)}) async-start(), calls=%async_computation.3 | async-start | bytes 1966080 | tf_op jit(solution)/shard_map/all_gather | solution.py:20
  68.9 22.0 %copy-start.3 = (bf16[512,384]{1,0:T(8,128)(2,1)S(1)}, bf16[512,384]{1,0:T(8,128)(2,1)}, u32[]{:S(2)}) copy-start(bf16[512,384]{1,0:T(8,128)(2,1)} %fusion.101) | copy-start | bytes 1179652
  74.7 13.1 %collective-permute-start.2 = (bf16[512,384]{1,0:T(8,128)(2,1)S(1)}, bf16[512,384]{1,0:T(8,128)(2,1)S(1)}, u32[]{:S(2)}, u32[]{:S(2)}) collective-permute-start(bf16[512,384]{1,0:T(8,128)(2,1)S(1)} %get-tuple-element.12), channel_id=1, source_target_pairs={{0,4},{4,8},{8,12},{1,5},{5,9},{9,13},{2,6},{6,10},{10,14},{3,7},{... | collective-permute-start | bytes 1179656 | tf_op jit(solution)/shard_map/ppermute | solution.py:15
  78.1 12.9 %collective-permute-start.3 = (bf16[512,384]{1,0:T(8,128)(2,1)S(1)}, bf16[512,384]{1,0:T(8,128)(2,1)S(1)}, u32[]{:S(2)}, u32[]{:S(2)}) collective-permute-start(bf16[512,384]{1,0:T(8,128)(2,1)S(1)} %get-tuple-element.13), channel_id=1, source_target_pairs={{4,0},{8,4},{12,8},{5,1},{9,5},{13,9},{6,2},{10,6},{14,10},{7,3},{... | collective-permute-start | bytes 1179656 | tf_op jit(solution)/shard_map/ppermute | solution.py:15
  91.9 71.0 %all-gather.13.cloned.1.call-start = ((), (), s32[]{:S(2)}) async-start(), calls=%async_computation.4 | async-start | bytes 1966080 | tf_op jit(solution)/shard_map/all_gather | solution.py:50
  112.6 27.2 %copy-start.4 = (bf16[512,384]{1,0:T(8,128)(2,1)S(1)}, bf16[512,384]{1,0:T(8,128)(2,1)}, u32[]{:S(2)}) copy-start(bf16[512,384]{1,0:T(8,128)(2,1)} %fusion.98) | copy-start | bytes 1179652
  118.4 21.5 %collective-permute-start.4 = (bf16[512,384]{1,0:T(8,128)(2,1)S(1)}, bf16[512,384]{1,0:T(8,128)(2,1)S(1)}, u32[]{:S(2)}, u32[]{:S(2)}) collective-permute-start(bf16[512,384]{1,0:T(8,128)(2,1)S(1)} %get-tuple-element.10), channel_id=1, source_target_pairs={{0,8},{4,12},{1,9},{5,13},{2,10},{6,14},{3,11},{7,15},{16,24},{20,... | collective-permute-start | bytes 1179656 | tf_op jit(solution)/shard_map/ppermute | solution.py:15
  122.7 17.1 %collective-permute-start.5 = (bf16[512,384]{1,0:T(8,128)(2,1)S(1)}, bf16[512,384]{1,0:T(8,128)(2,1)S(1)}, u32[]{:S(2)}, u32[]{:S(2)}) collective-permute-start(bf16[512,384]{1,0:T(8,128)(2,1)S(1)} %get-tuple-element.11), channel_id=1, source_target_pairs={{8,0},{12,4},{9,1},{13,5},{10,2},{14,6},{11,3},{15,7},{24,16},{28,... | collective-permute-start | bytes 1179656 | tf_op jit(solution)/shard_map/ppermute | solution.py:15
  140.8 57.0 %all-gather.15.cloned.1.call-start = ((), (), s32[]{:S(2)}) async-start(), calls=%async_computation.5 | async-start | bytes 2359296 | tf_op jit(solution)/shard_map/all_gather | solution.py:76
  140.9 27.8 %copy-start.5 = (bf16[512,1536]{1,0:T(8,128)(2,1)S(1)}, bf16[512,1536]{1,0:T(8,128)(2,1)}, u32[]{:S(2)}) copy-start(bf16[512,1536]{1,0:T(8,128)(2,1)} %param.13) | copy-start | bytes 4718596
  165.4 62.9 %all-gather.17.cloned.1.call-start = ((), (), s32[]{:S(2)}) async-start(), calls=%async_computation.6 | async-start | bytes 2359296 | tf_op jit(solution)/shard_map/all_gather | solution.py:77
  170.3 23.6 %all-to-all-start = ((bf16[512,2,768]{0,2,1:T(8,128)(2,1)}), bf16[512,2,768]{0,2,1:T(8,128)(2,1)S(1)}, u32[]{:S(2)}, u32[]{:S(2)}) async-start(bf16[512,2,768]{0,2,1:T(8,128)(2,1)} %bitcast.118), calls=%async_computation | async-start | bytes 3145728 | tf_op jit(solution)/shard_map/all_to_all | solution.py:95
  200.7 3.2 %copy-start.1 = (f32[4,256,2048]{2,1,0:T(8,128)}, f32[4,256,2048]{2,1,0:T(8,128)S(1)}, u32[]{:S(2)}) copy-start(f32[4,256,2048]{2,1,0:T(8,128)S(1)} %get-tuple-element.25) | copy-start | bytes 25165828
  228.3 15.1 %copy-start.2 = (bf16[2,512,768]{2,1,0:T(8,128)(2,1)S(1)}, bf16[2,512,768]{2,1,0:T(8,128)(2,1)}, u32[]{:S(2)}) copy-start(bf16[2,512,768]{2,1,0:T(8,128)(2,1)} %copy.18) | copy-start | bytes 4718596
Sparse Core Ops, SparseCore 0:
  8.9 20.7 all-gather.6
  48.4 18.7 all-gather.8
  92.1 18.7 all-gather.10
  140.9 21.9 all-gather.12
  165.5 29.0 all-gather.14
  196.1 32.1 all-gather.16
where the time goes:
time: 253 us
  waiting for transfers between devices  155 us (61%)
  matrix products  34.3 us (14%)
  starting transfers between devices  21.6 us (9%)
  between operations  13.7 us (5%)
  other arithmetic  9.91 us (4%)
  local copies, waits for them, and re-layouts  9.22 us (4%)
  blocking collectives  9.14 us (4%)
    all_gather x3, waiting for transfers between devices, tower_section(): gathered = lax.all_gather(stream_shard, ('mp', 'sub'), axis=1, tiled=True)  59.2 us
    ppermute x6, waiting for transfers between devices, passed_along(): return lax.ppermute(x, axis, pairs)  30.2 us
    all_gather x1, waiting for transfers between devices, per_device(): value_rows = lax.all_gather(values, ('seq', 'sub'), axis=0, tiled=True)  22.7 us
    all_gather x1, waiting for transfers between devices, per_device(): widest = lax.all_gather(stream, ('mp', 'sub'), axis=1, tiled=True)  22 us
    all_to_all x1, waiting for transfers between devices, per_device(): lax.all_to_all(w_o, 'mp', split_axis=1, concat_axis=0, tiled=True)  19.9 us
    ppermute x6, starting transfers between devices, passed_along(): return lax.ppermute(x, axis, pairs)  17.5 us
    dot_general x3, matrix products, tower_section(): jnp.einsum('rc,jco->jro', hidden, weight_taps, preferred_element_type=jnp...  16.9 us
    all_gather x1, blocking collectives, per_device(): every_head = lax.all_gather(attended, 'mp', axis=1, tiled=True)  9.14 us
  transfers between devices with their start and end apart: 13, of which 11 were waited for; matrix products, arithmetic and copies ran while one was open for 6% of the time, Pallas kernels for 0%

commit v1 on v0

--- a/solution.py
+++ b/solution.py
@@ -73,8 +73,11 @@
     score_scale = 1.0 / math.sqrt(HEAD)
     running_top = jnp.full((heads_here, query_rows), -1e30, jnp.float32)
     running_numer = jnp.zeros((query_rows, heads_here, HEAD), jnp.float32)
-    key_rows = lax.all_gather(keys, ("seq", "sub"), axis=0, tiled=True)
-    value_rows = lax.all_gather(values, ("seq", "sub"), axis=0, tiled=True)
+    key_rows, value_rows = jnp.split(
+        lax.all_gather(jnp.concatenate([keys, values], axis=1), ("seq", "sub"), axis=0, tiled=True),
+        [keys.shape[1]],
+        axis=1,
+    )
     scores = (
         jnp.einsum("qhe,khe->hqk", queries, key_rows, preferred_element_type=jnp.float32)
         * score_scale

time: 253 us -> 243 us (0.960); the launches traced: 253 us -> 239 us
  waiting for transfers between devices: 155 us -> 149 us
  local copies, waits for them, and re-layouts: 9.22 us -> 4.99 us
  matrix products: 34.3 us -> 30.4 us
    all_gather x2 -> x1, waiting for transfers between devices: 22.7 us -> 16.8 us  [per_device(): lax.all_gather(jnp.concatenate([keys, values], axis=1), ('seq', 'sub'), a...]
    dot_general x1, matrix products: 5.95 us -> 1.99 us  [per_device(): jnp.einsum('hqk,khe->qhe', expw.astype(jnp.bfloat16), value_rows, preferr...]
    unnamed x15, local copies, waits for them, and re-layouts: 4.83 us -> 2.16 us
  transfers between devices with their start and end apart: 13 -> 12, of which waited for: 11 -> 11; matrix products, arithmetic and copies ran while one was open for 6% -> 3% of each run, Pallas kernels for 0% -> 0%
where the time goes in v1:
time: 243 us; the launch traced here: 239 us
  waiting for transfers between devices  149 us (61%)
  matrix products  30.4 us (13%)
  starting transfers between devices  21.5 us (9%)
  between operations  13.4 us (6%)
  other arithmetic  10.8 us (4%)
  blocking collectives  9.13 us (4%)
  local copies, waits for them, and re-layouts  4.99 us (2%)
    all_gather x3, waiting for transfers between devices, tower_section(): gathered = lax.all_gather(stream_shard, ('mp', 'sub'), axis=1, tiled=True)  59.2 us
    ppermute x6, waiting for transfers between devices, passed_along(): return lax.ppermute(x, axis, pairs)  30.2 us
    all_gather x1, waiting for transfers between devices, per_device(): widest = lax.all_gather(stream, ('mp', 'sub'), axis=1, tiled=True)  21.8 us
    all_to_all x1, waiting for transfers between devices, per_device(): lax.all_to_all(w_o, 'mp', split_axis=1, concat_axis=0, tiled=True)  19.9 us
    ppermute x6, starting transfers between devices, passed_along(): return lax.ppermute(x, axis, pairs)  17.5 us
    dot_general x3, matrix products, tower_section(): jnp.einsum('rc,jco->jro', hidden, weight_taps, preferred_element_type=jnp...  16.9 us
    all_gather x1, waiting for transfers between devices, per_device(): lax.all_gather(jnp.concatenate([keys, values], axis=1), ('seq', 'sub'), a...  16.8 us
    all_gather x1, blocking collectives, per_device(): every_head = lax.all_gather(attended, 'mp', axis=1, tiled=True)  9.13 us
  transfers between devices with their start and end apart: 12, of which 11 were waited for; matrix products, arithmetic and copies ran while one was open for 3% of the time, Pallas kernels for 0%

profile of v1, /device:TPU:8, one launch (start us, length us, event | category | flops | bytes accessed | tf_op | source)
XLA Modules:
  0.0 238.9 jit_solution(10739785744846522790)
XLA Ops:
  6.5 0.0 copy-start
  6.5 0.0 all-gather.6.cloned.1.call-start
  6.5 0.7 all-gather.6.cloned.1.call-update
  7.3 0.0 all-gather.8.cloned.1.call-start
  7.3 0.9 slice_reduce_fusion
  8.2 21.5 %all-gather.6.cloned.1.call-done = bf16[512,1536]{1,0:T(8,128)(2,1)} async-done(((bf16[512,384]{1,0:T(8,128)(2,1)}), bf16[512,1536]{1,0:T(8,128)(2,1)}) %all-gather.6.cloned.1.call-update) | async-done | bytes 1572880 | tf_op jit(solution)/shard_map/all_gather | solution.py:20
  29.8 1.8 fusion.15
  31.6 5.6 %fusion.126 = (bf16[3,512,384]{2,1,0:T(8,128)(2,1)S(1)}, f32[3,512,384]{2,1,0:T(8,128)S(1)}) fusion(bf16[3,3,1536,384]{3,2,1,0:T(8,128)(2,1)} %param.9, bf16[512,1536]{1,0:T(8,128)(2,1)} %all-gather.6.cloned.1.call-done, f32[1536]{0:T(1024)S(1)} %get-tuple-element.6, f32[512]{0:T(512)S(1)} %add_rsqrt_fusion.2), kind=kOutput, calls=%fused_computation.146 | convolution fusion | flops 1821966336 | bytes 8658944 | tf_op jit(solution)/shard_map/rc,jco->jro/dot_general | solution.py:26
  37.1 0.0 copy-start.5
  37.2 3.5 %collective-permute-start = (bf16[128,384]{1,0:T(8,128)(2,1)S(1)}, bf16[128,384]{1,0:T(8,128)(2,1)S(1)}, u32[]{:S(2)}, u32[]{:S(2)}) collective-permute-start(bf16[128,384]{1,0:T(8,128)(2,1)S(1)} %get-tuple-element.15), channel_id=1, source_target_pairs={{0,4},{4,8},{8,12},{1,5},{5,9},{9,13},{2,6},{6,10},{10,14},{3,7},{... | collective-permute-start | bytes 294920 | tf_op jit(solution)/shard_map/ppermute | solution.py:15
  40.7 2.5 %collective-permute-start.1 = (bf16[128,384]{1,0:T(8,128)(2,1)S(1)}, bf16[128,384]{1,0:T(8,128)(2,1)S(1)}, u32[]{:S(2)}, u32[]{:S(2)}) collective-permute-start(bf16[128,384]{1,0:T(8,128)(2,1)S(1)} %get-tuple-element.14), channel_id=1, source_target_pairs={{4,0},{8,4},{12,8},{5,1},{9,5},{13,9},{6,2},{10,6},{14,10},{7,3},{... | collective-permute-start | bytes 294920 | tf_op jit(solution)/shard_map/ppermute | solution.py:15
  43.2 0.1 slice_bitcast_fusion.3
  43.3 0.9 collective-permute-done
  44.2 3.1 %collective-permute-done.1 = bf16[128,384]{1,0:T(8,128)(2,1)S(1)} collective-permute-done((bf16[128,384]{1,0:T(8,128)(2,1)S(1)}, bf16[128,384]{1,0:T(8,128)(2,1)S(1)}, u32[]{:S(2)}, u32[]{:S(2)}) %collective-permute-start.1) | collective-permute-done | bytes 98336 | tf_op jit(solution)/shard_map/ppermute | solution.py:15
  47.3 0.0 copy-done.5
  47.3 0.9 fusion.104
  48.2 0.0 all-gather.8.cloned.1.call-update
  48.3 0.0 all-gather.10.cloned.1.call-start
  48.3 18.8 %all-gather.8.cloned.1.call-done = bf16[512,1536]{1,0:T(8,128)(2,1)} async-done(((bf16[512,384]{1,0:T(8,128)(2,1)}), bf16[512,1536]{1,0:T(8,128)(2,1)}) %all-gather.8.cloned.1.call-update) | async-done | bytes 1572880 | tf_op jit(solution)/shard_map/all_gather | solution.py:20
  67.1 1.8 fusion.24
  68.9 0.0 copy-start.2
  68.9 5.6 %fusion.127 = (bf16[3,512,384]{2,1,0:T(8,128)(2,1)S(1)}, f32[3,512,384]{2,1,0:T(8,128)S(1)}) fusion(bf16[3,3,1536,384]{3,2,1,0:T(8,128)(2,1)} %param.9, bf16[512,1536]{1,0:T(8,128)(2,1)} %all-gather.8.cloned.1.call-done, f32[1536]{0:T(1024)S(1)} %get-tuple-element.7, f32[512]{0:T(512)S(1)} %add_rsqrt_fusion.1), kind=kOutput, calls=%fused_computation.147 | convolution fusion | flops 1821966336 | bytes 8658944 | tf_op jit(solution)/shard_map/rc,jco->jro/dot_general | solution.py:26
  74.6 0.1 slice_bitcast_fusion.8
  74.7 3.4 %collective-permute-start.2 = (bf16[512,384]{1,0:T(8,128)(2,1)S(1)}, bf16[512,384]{1,0:T(8,128)(2,1)S(1)}, u32[]{:S(2)}, u32[]{:S(2)}) collective-permute-start(bf16[512,384]{1,0:T(8,128)(2,1)S(1)} %get-tuple-element.12), channel_id=1, source_target_pairs={{0,4},{4,8},{8,12},{1,5},{5,9},{9,13},{2,6},{6,10},{10,14},{3,7},{... | collective-permute-start | bytes 1179656 | tf_op jit(solution)/shard_map/ppermute | solution.py:15
  78.1 2.5 %collective-permute-start.3 = (bf16[512,384]{1,0:T(8,128)(2,1)S(1)}, bf16[512,384]{1,0:T(8,128)(2,1)S(1)}, u32[]{:S(2)}, u32[]{:S(2)}) collective-permute-start(bf16[512,384]{1,0:T(8,128)(2,1)S(1)} %get-tuple-element.13), channel_id=1, source_target_pairs={{4,0},{8,4},{12,8},{5,1},{9,5},{13,9},{6,2},{10,6},{14,10},{7,3},{... | collective-permute-start | bytes 1179656 | tf_op jit(solution)/shard_map/ppermute | solution.py:15
  80.6 7.3 %collective-permute-done.2 = bf16[512,384]{1,0:T(8,128)(2,1)S(1)} collective-permute-done((bf16[512,384]{1,0:T(8,128)(2,1)S(1)}, bf16[512,384]{1,0:T(8,128)(2,1)S(1)}, u32[]{:S(2)}, u32[]{:S(2)}) %collective-permute-start.2) | collective-permute-done | bytes 393248 | tf_op jit(solution)/shard_map/ppermute | solution.py:15
  87.8 3.1 %collective-permute-done.3 = bf16[512,384]{1,0:T(8,128)(2,1)S(1)} collective-permute-done((bf16[512,384]{1,0:T(8,128)(2,1)S(1)}, bf16[512,384]{1,0:T(8,128)(2,1)S(1)}, u32[]{:S(2)}, u32[]{:S(2)}) %collective-permute-start.3) | collective-permute-done | bytes 393248 | tf_op jit(solution)/shard_map/ppermute | solution.py:15
  90.9 0.0 copy-done.2
  90.9 1.0 fusion.101
  91.9 0.0 all-gather.10.cloned.1.call-update
  91.9 0.0 all-gather.12.cloned.1.call-start
  92.0 18.8 %all-gather.10.cloned.1.call-done = bf16[512,1536]{1,0:T(8,128)(2,1)} async-done(((bf16[512,384]{1,0:T(8,128)(2,1)}), bf16[512,1536]{1,0:T(8,128)(2,1)}) %all-gather.10.cloned.1.call-update) | async-done | bytes 1572880 | tf_op jit(solution)/shard_map/all_gather | solution.py:20
  110.8 1.8 fusion.33
  112.6 0.0 copy-start.3
  112.6 5.6 %fusion.128 = (bf16[3,512,384]{2,1,0:T(8,128)(2,1)S(1)}, f32[3,512,384]{2,1,0:T(8,128)S(1)}) fusion(bf16[3,3,1536,384]{3,2,1,0:T(8,128)(2,1)} %param.9, bf16[512,1536]{1,0:T(8,128)(2,1)} %all-gather.10.cloned.1.call-done, f32[1536]{0:T(1024)S(1)} %get-tuple-element.5, f32[512]{0:T(512)S(1)} %add_rsqrt_fusion), kind=kOutput, calls=%fused_computation.148 | convolution fusion | flops 1821966336 | bytes 8658944 | tf_op jit(solution)/shard_map/rc,jco->jro/dot_general | solution.py:26
  118.3 0.1 slice_bitcast_fusion.6
  118.4 4.3 %collective-permute-start.4 = (bf16[512,384]{1,0:T(8,128)(2,1)S(1)}, bf16[512,384]{1,0:T(8,128)(2,1)S(1)}, u32[]{:S(2)}, u32[]{:S(2)}) collective-permute-start(bf16[512,384]{1,0:T(8,128)(2,1)S(1)} %get-tuple-element.10), channel_id=1, source_target_pairs={{0,8},{4,12},{1,9},{5,13},{2,10},{6,14},{3,11},{7,15},{16,24},{20,... | collective-permute-start | bytes 1179656 | tf_op jit(solution)/shard_map/ppermute | solution.py:15
  122.7 1.3 collective-permute-start.5
  124.0 15.8 %collective-permute-done.4 = bf16[512,384]{1,0:T(8,128)(2,1)S(1)} collective-permute-done((bf16[512,384]{1,0:T(8,128)(2,1)S(1)}, bf16[512,384]{1,0:T(8,128)(2,1)S(1)}, u32[]{:S(2)}, u32[]{:S(2)}) %collective-permute-start.4) | collective-permute-done | bytes 393248 | tf_op jit(solution)/shard_map/ppermute | solution.py:15
  139.8 0.0 collective-permute-done.5
  139.8 0.0 copy-done.3
  139.8 1.0 fusion.98
  140.8 0.0 all-gather.12.cloned.1.call-update
  140.8 0.2 all-gather.14.cloned.1.call-start
  141.1 21.8 %all-gather.12.cloned.1.call-done = bf16[512,1536]{1,0:T(8,128)(2,1)} async-done(((bf16[512,384]{1,0:T(8,128)(2,1)}), bf16[512,1536]{1,0:T(8,128)(2,1)}) %all-gather.12.cloned.1.call-update) | async-done | bytes 1572880 | tf_op jit(solution)/shard_map/all_gather | solution.py:50
  162.9 0.0 copy-done
  162.9 1.7 fusion.94
  164.6 0.0 copy-start.4
  164.6 2.3 fusion.95
  167.0 0.1 copy_bitcast_fusion
  167.1 0.8 pad_maximum_fusion
  167.9 0.0 all-gather.14.cloned.1.call-update
  167.9 1.6 copy.20
  169.5 3.7 %all-to-all-start = ((bf16[512,2,768]{0,2,1:T(8,128)(2,1)}), bf16[512,2,768]{0,2,1:T(8,128)(2,1)S(1)}, u32[]{:S(2)}, u32[]{:S(2)}) async-start(bf16[512,2,768]{0,2,1:T(8,128)(2,1)} %bitcast.119), calls=%async_computation | async-start | bytes 3145728 | tf_op jit(solution)/shard_map/all_to_all | solution.py:98
  173.2 19.9 %all-to-all-done = bf16[512,2,768]{0,2,1:T(8,128)(2,1)S(1)} async-done(((bf16[512,2,768]{0,2,1:T(8,128)(2,1)}), bf16[512,2,768]{0,2,1:T(8,128)(2,1)S(1)}, u32[]{:S(2)}, u32[]{:S(2)}) %all-to-all-start) | async-done | bytes 1572896 | tf_op jit(solution)/shard_map/all_to_all | solution.py:98
  193.1 1.6 copy.21
  194.7 2.2 fusion.93
  196.9 16.8 %all-gather.14.cloned.1.call-done = bf16[2048,8,128]{2,0,1:T(8,128)(2,1)} async-done(((bf16[256,8,128]{2,0,1:T(8,128)(2,1)}), bf16[2048,8,128]{2,0,1:T(8,128)(2,1)}) %all-gather.14.cloned.1.call-update) | async-done | bytes 4194320 | tf_op jit(solution)/shard_map/all_gather | solution.py:77
  213.7 2.9 %multiply_reduce_fusion = (f32[4,256]{1,0:T(4,128)S(1)}, f32[4,256,2048]{2,1,0:T(8,128)S(1)}) fusion(bf16[2048,8,128]{2,0,1:T(8,128)(2,1)} %all-gather.14.cloned.1.call-done, bf16[32,4,8,128]{3,2,1,0:T(8,128)(2,1)S(1)} %fusion.93), kind=kOutput, calls=%fused_computation.1 | convolution fusion | flops 541064192 | bytes 10752000 | tf_op jit(solution)/shard_map/qhe,khe->hqk/dot_general | solution.py:82
  216.6 1.6 fusion
  218.3 0.5 copy-done.6
  218.8 2.0 fusion.90
  220.8 9.1 %all_gather.23 = bf16[256,1024]{0,1:T(8,128)(2,1)S(1)} all-gather(bf16[256,512]{0,1:T(8,128)(2,1)S(1)} %bitcast.121), channel_id=1, replica_groups=mesh['groups'=2,'seq'=4,'mp'=2,'sub'=2] {'mp'}, dimensions={1}, use_global_device_ids=true | all-gather | bytes 786432 | tf_op jit(solution)/shard_map/all_gather | solution.py:99
  229.9 2.4 %fusion.80 = bf16[256,768]{1,0:T(8,128)(2,1)} fusion(bf16[256,1024]{0,1:T(8,128)(2,1)S(1)} %all_gather.23, bf16[1024,768]{1,0:T(8,128)(2,1)S(1)} %bitcast.120, bf16[512,1536]{1,0:T(8,128)(2,1)} %all-gather.12.cloned.1.call-done, s32[]{:T(128)S(6)} %select_n.11, s32[]{:T(128)S(6)} %select_n.13), kind=kOutput, calls=%fused_computation.82 | convolution fusion | flops 403243008 | bytes 2883592 | tf_op jit(solution)/shard_map/dot_general | solution.py:100
  (11 shorter events, 0.1 us)
Async XLA Ops:
  6.5 156.4 %copy-start = (bf16[1536,512]{1,0:T(8,128)(2,1)S(1)}, bf16[1536,512]{1,0:T(8,128)(2,1)}, u32[]{:S(2)}) copy-start(bf16[1536,512]{1,0:T(8,128)(2,1)} %param.11) | copy-start | bytes 4718596
  6.5 23.2 %all-gather.6.cloned.1.call-start = ((), (), s32[]{:S(2)}) async-start(), calls=%async_computation.1 | async-start | bytes 1966080 | tf_op jit(solution)/shard_map/all_gather | solution.py:20
  7.3 59.9 %all-gather.8.cloned.1.call-start = ((), (), s32[]{:S(2)}) async-start(), calls=%async_computation.2 | async-start | bytes 1966080 | tf_op jit(solution)/shard_map/all_gather | solution.py:20
  37.1 10.1 %copy-start.5 = (bf16[512,384]{1,0:T(8,128)(2,1)S(1)}, bf16[512,384]{1,0:T(8,128)(2,1)}, u32[]{:S(2)}) copy-start(bf16[512,384]{1,0:T(8,128)(2,1)} %param.7) | copy-start | bytes 1179652
  37.2 7.0 %collective-permute-start = (bf16[128,384]{1,0:T(8,128)(2,1)S(1)}, bf16[128,384]{1,0:T(8,128)(2,1)S(1)}, u32[]{:S(2)}, u32[]{:S(2)}) collective-permute-start(bf16[128,384]{1,0:T(8,128)(2,1)S(1)} %get-tuple-element.15), channel_id=1, source_target_pairs={{0,4},{4,8},{8,12},{1,5},{5,9},{9,13},{2,6},{6,10},{10,14},{3,7},{... | collective-permute-start | bytes 294920 | tf_op jit(solution)/shard_map/ppermute | solution.py:15
  40.7 6.6 %collective-permute-start.1 = (bf16[128,384]{1,0:T(8,128)(2,1)S(1)}, bf16[128,384]{1,0:T(8,128)(2,1)S(1)}, u32[]{:S(2)}, u32[]{:S(2)}) collective-permute-start(bf16[128,384]{1,0:T(8,128)(2,1)S(1)} %get-tuple-element.14), channel_id=1, source_target_pairs={{4,0},{8,4},{12,8},{5,1},{9,5},{13,9},{6,2},{10,6},{14,10},{7,3},{... | collective-permute-start | bytes 294920 | tf_op jit(solution)/shard_map/ppermute | solution.py:15
  48.3 62.5 %all-gather.10.cloned.1.call-start = ((), (), s32[]{:S(2)}) async-start(), calls=%async_computation.3 | async-start | bytes 1966080 | tf_op jit(solution)/shard_map/all_gather | solution.py:20
  68.9 22.0 %copy-start.2 = (bf16[512,384]{1,0:T(8,128)(2,1)S(1)}, bf16[512,384]{1,0:T(8,128)(2,1)}, u32[]{:S(2)}) copy-start(bf16[512,384]{1,0:T(8,128)(2,1)} %fusion.104) | copy-start | bytes 1179652
  74.7 13.1 %collective-permute-start.2 = (bf16[512,384]{1,0:T(8,128)(2,1)S(1)}, bf16[512,384]{1,0:T(8,128)(2,1)S(1)}, u32[]{:S(2)}, u32[]{:S(2)}) collective-permute-start(bf16[512,384]{1,0:T(8,128)(2,1)S(1)} %get-tuple-element.12), channel_id=1, source_target_pairs={{0,4},{4,8},{8,12},{1,5},{5,9},{9,13},{2,6},{6,10},{10,14},{3,7},{... | collective-permute-start | bytes 1179656 | tf_op jit(solution)/shard_map/ppermute | solution.py:15
  78.1 12.9 %collective-permute-start.3 = (bf16[512,384]{1,0:T(8,128)(2,1)S(1)}, bf16[512,384]{1,0:T(8,128)(2,1)S(1)}, u32[]{:S(2)}, u32[]{:S(2)}) collective-permute-start(bf16[512,384]{1,0:T(8,128)(2,1)S(1)} %get-tuple-element.13), channel_id=1, source_target_pairs={{4,0},{8,4},{12,8},{5,1},{9,5},{13,9},{6,2},{10,6},{14,10},{7,3},{... | collective-permute-start | bytes 1179656 | tf_op jit(solution)/shard_map/ppermute | solution.py:15
  91.9 71.0 %all-gather.12.cloned.1.call-start = ((), (), s32[]{:S(2)}) async-start(), calls=%async_computation.4 | async-start | bytes 1966080 | tf_op jit(solution)/shard_map/all_gather | solution.py:50
  112.6 27.2 %copy-start.3 = (bf16[512,384]{1,0:T(8,128)(2,1)S(1)}, bf16[512,384]{1,0:T(8,128)(2,1)}, u32[]{:S(2)}) copy-start(bf16[512,384]{1,0:T(8,128)(2,1)} %fusion.101) | copy-start | bytes 1179652
  118.4 21.5 %collective-permute-start.4 = (bf16[512,384]{1,0:T(8,128)(2,1)S(1)}, bf16[512,384]{1,0:T(8,128)(2,1)S(1)}, u32[]{:S(2)}, u32[]{:S(2)}) collective-permute-start(bf16[512,384]{1,0:T(8,128)(2,1)S(1)} %get-tuple-element.10), channel_id=1, source_target_pairs={{0,8},{4,12},{1,9},{5,13},{2,10},{6,14},{3,11},{7,15},{16,24},{20,... | collective-permute-start | bytes 1179656 | tf_op jit(solution)/shard_map/ppermute | solution.py:15
  122.7 17.1 %collective-permute-start.5 = (bf16[512,384]{1,0:T(8,128)(2,1)S(1)}, bf16[512,384]{1,0:T(8,128)(2,1)S(1)}, u32[]{:S(2)}, u32[]{:S(2)}) collective-permute-start(bf16[512,384]{1,0:T(8,128)(2,1)S(1)} %get-tuple-element.11), channel_id=1, source_target_pairs={{8,0},{12,4},{9,1},{13,5},{10,2},{14,6},{11,3},{15,7},{24,16},{28,... | collective-permute-start | bytes 1179656 | tf_op jit(solution)/shard_map/ppermute | solution.py:15
  140.8 72.8 %all-gather.14.cloned.1.call-start = ((), (), s32[]{:S(2)}) async-start(), calls=%async_computation.5 | async-start | bytes 4718592 | tf_op jit(solution)/shard_map/all_gather | solution.py:77
  164.6 3.3 %copy-start.4 = (bf16[512,1536]{1,0:T(8,128)(2,1)S(1)}, bf16[512,1536]{1,0:T(8,128)(2,1)}, u32[]{:S(2)}) copy-start(bf16[512,1536]{1,0:T(8,128)(2,1)} %param.13) | copy-start | bytes 4718596
  169.5 23.6 %all-to-all-start = ((bf16[512,2,768]{0,2,1:T(8,128)(2,1)}), bf16[512,2,768]{0,2,1:T(8,128)(2,1)S(1)}, u32[]{:S(2)}, u32[]{:S(2)}) async-start(bf16[512,2,768]{0,2,1:T(8,128)(2,1)} %bitcast.119), calls=%async_computation | async-start | bytes 3145728 | tf_op jit(solution)/shard_map/all_to_all | solution.py:98
  216.6 2.2 copy-start.6
  218.8 11.1 %copy-start.1 = (bf16[2,512,768]{2,1,0:T(8,128)(2,1)S(1)}, bf16[2,512,768]{2,1,0:T(8,128)(2,1)}, u32[]{:S(2)}) copy-start(bf16[2,512,768]{2,1,0:T(8,128)(2,1)} %copy.21) | copy-start | bytes 4718596
Sparse Core Ops, SparseCore 0:
  8.9 20.7 all-gather.5
  48.4 18.7 all-gather.7
  92.1 18.7 all-gather.9
  140.9 21.9 all-gather.11
  168.1 45.5 all-gather.13
